TPU v7x, 32 devices: a whole 2x2x4 slice. The times are simulated.
32 devices in a mesh: ckpt: 2 (over y), row: 16 (over z, x, core).
Axes of the slice: x: 2, y: 2, z: 4, core: 2. Of those that a mesh axis runs over, the one named last changes fastest.
Arguments:
- activations: bfloat16 [4096, 4096], P(('ckpt', 'row')), parts along dimension 0, may hold values from -6 to 6
- gate_pre: bfloat16 [4096, 7168], P(('ckpt', 'row')), parts along dimension 0, may hold values from -8 to 8
- out_grad: bfloat16 [4096, 4096], P(('ckpt', 'row')), parts along dimension 0, may hold values from -6 to 6
- down_weight: bfloat16 [14336, 4096], P(('ckpt', 'row')), parts along dimension 0, may hold values from -0.09375 to 0.09375
- proj_in: bfloat16 [4096, 64], replicated, may hold values from -0.09375 to 0.09375
- proj_out: bfloat16 [7168, 64], replicated, may hold values from -0.0625 to 0.0625
- stored: bfloat16 [24576, 4096], P(('ckpt', 'row')), parts along dimension 0, may hold values from -0.09375 to 0.09375
- visible: int32 [16], replicated, may hold values from 1 to 12288, as said below
Outputs:
- scores: float32 [32, 12288], P('ckpt', 'row'), parts along dimension 0
There are 2 independent parts, one for each index of `ckpt`. A program takes and returns all parts, laid end to end along the dimension named above; an argument that names none is the same for every part. Nothing has to cross between parts.
Inputs may be any that keep to these rules, and one draw needn't show every extreme that they name: `visible`: some query example sees all 12288 stored examples and some sees exactly one.
All inputs are finite; a program needn't handle non-finite values.
Results may differ from a plain program's by a relative error of at most 0.0064.
Values may be sent and summed in bfloat16 or wider, within the bound.
No kernel may reach another device: no remote copies, remote signals or barrier semaphores. Data moves between devices by JAX's collectives and lax.ppermute only.
A program may use at most 128 MiB of HBM per device.

v0:
```python
import jax
import jax.numpy as jnp
from jax import lax
from jax.sharding import PartitionSpec as P

SEQ_LEN = 128


def partner(value, axis, bit):
    return lax.ppermute(value, axis, [(i, i ^ 1 << bit) for i in range(lax.axis_size(axis))])


def collect(pieces, position, bit_list, sender):
    for bit_level in bit_list:
        partner_rows = sender(pieces, bit_level)
        upper_half = position >> bit_level & 1 == 1
        pieces = jnp.where(
            upper_half,
            jnp.concatenate([partner_rows, pieces], axis=0),
            jnp.concatenate([pieces, partner_rows], axis=0),
        )
    return pieces


def xor_order(slot_data, lane_id, lane_bits):
    lane_total = 1 << lane_bits
    for bit_level in range(lane_bits):
        shaped = slot_data.reshape(
            (lane_total >> bit_level + 1, 2, 1 << bit_level) + slot_data.shape[1:]
        )
        flipped = shaped[:, ::-1].reshape(slot_data.shape)
        slot_data = jnp.where(lane_id >> bit_level & 1 == 1, flipped, slot_data)
    return slot_data


def lane_exchange(slot_data, lane_id, lane_bits):
    lane_total = 1 << lane_bits
    slot_data = xor_order(slot_data, lane_id, lane_bits)
    for bit_level in range(lane_bits):
        shaped = slot_data.reshape(
            (lane_total >> bit_level + 1, 2, 1 << bit_level) + slot_data.shape[1:]
        )
        arrived = partner(shaped[:, 1], "row", bit_level)
        slot_data = jnp.concatenate([shaped[:, :1], arrived[:, None]], axis=1).reshape(
            slot_data.shape
        )
    return xor_order(slot_data, lane_id, lane_bits)


def shards(activations, gate_pre, out_grad, down_weight, proj_in, proj_out, stored, visible):
    devices = lax.axis_size("row")
    position = lax.axis_index("row")
    total_bits = devices.bit_length() - 1
    lane_bits = 3
    lane_total = 1 << lane_bits
    lane_id = position % lane_total
    tokens_dev = activations.shape[0]
    hidden_total = gate_pre.shape[1]
    rows_piece = down_weight.shape[0]
    groups = hidden_total // (rows_piece * lane_total)
    rank_size = proj_in.shape[1]
    weights_lane = collect(
        down_weight,
        position,
        range(lane_bits, total_bits),
        lambda pieces, bit_level: partner(pieces, "row", bit_level),
    )
    grad_group = collect(
        out_grad,
        position,
        range(0, lane_bits),
        lambda pieces, bit_level: partner(pieces, "row", bit_level),
    )
    hidden_block = lax.dot_general(
        grad_group, weights_lane, (((1,), (1,)), ((), ())), preferred_element_type=jnp.float32
    ).astype(jnp.bfloat16)
    received = lane_exchange(
        hidden_block.reshape(lane_total, tokens_dev, groups * rows_piece), lane_id, lane_bits
    )
    full_grad = (
        received.reshape(lane_total, tokens_dev, groups, rows_piece)
        .transpose(1, 2, 0, 3)
        .reshape(tokens_dev, hidden_total)
    )
    up_grad = (
        lax.optimization_barrier(full_grad).astype(jnp.float32)
        * jax.nn.silu(gate_pre.astype(jnp.float32))
    ).astype(jnp.bfloat16)
    out_proj = jnp.dot(up_grad, proj_out, preferred_element_type=jnp.float32).astype(jnp.bfloat16)
    in_proj = jnp.dot(activations, proj_in, preferred_element_type=jnp.float32).astype(jnp.bfloat16)
    examples_dev = tokens_dev // SEQ_LEN
    in_split = in_proj.astype(jnp.float32).reshape(examples_dev, SEQ_LEN, rank_size)
    out_split = out_proj.astype(jnp.float32).reshape(examples_dev, SEQ_LEN, rank_size)
    raw_feature = jnp.einsum(
        "esa,esb->eab", in_split, out_split, preferred_element_type=jnp.float32
    ).reshape(examples_dev, rank_size * rank_size)
    scale = lax.rsqrt(jnp.mean(raw_feature * raw_feature, axis=1, keepdims=True) + 1e-06)
    queries = (raw_feature * scale).astype(jnp.bfloat16)
    stored_rows = stored.shape[0]
    column = position * stored_rows + jnp.arange(stored_rows, dtype=jnp.int32)
    products = lax.dot_general(
        lax.all_gather(queries, "row", axis=0, tiled=True),
        stored,
        (((1,), (1,)), ((), ())),
        preferred_element_type=jnp.float32,
    )
    return jnp.where(column[None, :] < visible[:, None], products, jnp.float32(0.0))


def solution(mesh):
    return jax.shard_map(
        shards,
        mesh=mesh,
        in_specs=(
            P(("ckpt", "row"), None),
            P(("ckpt", "row"), None),
            P(("ckpt", "row"), None),
            P(("ckpt", "row"), None),
            P(),
            P(),
            P(("ckpt", "row"), None),
            P(),
        ),
        out_specs=P("ckpt", "row"),
        check_vma=False,
    )
```

profile of v0, /device:TPU:0, one launch (start us, length us, event | category | flops | bytes accessed | tf_op | source)
XLA Modules:
  0.0 381.6 jit_solution(10606979016936965666)
XLA Ops:
  0.0 0.5 collective-permute-start
  0.5 2.6 collective-permute-done
  3.1 3.1 maximum_select_fusion.5
  6.2 2.9 collective-permute-start.1
  9.2 46.0 %collective-permute-done.1 = bf16[256,4096]{1,0:T(8,128)(2,1)} collective-permute-done((bf16[256,4096]{1,0:T(8,128)(2,1)S(1)}, bf16[256,4096]{1,0:T(8,128)(2,1)}, u32[]{:S(2)}, u32[]{:S(2)}) %collective-permute-start.1) | collective-permute-done | bytes 2097184 | tf_op jit(solution)/shard_map/ppermute | solution.py:10
  55.2 4.7 %maximum_select_fusion.4 = bf16[512,4096]{1,0:T(8,128)(2,1)} fusion(bf16[256,4096]{1,0:T(8,128)(2,1)S(1)} %maximum_select_fusion.5, bf16[256,4096]{1,0:T(8,128)(2,1)} %collective-permute-done.1, pred[]{:T(512)S(6)} %eq.30), kind=kLoop, calls=%fused_computation.17 | loop fusion | flops 18874368 | bytes 8388609 | tf_op jit(solution)/shard_map/jit(_where)/select_n | solution.py:17
  59.9 1.8 collective-permute-start.2
  61.8 2.6 collective-permute-start.3
  64.4 165.7 %collective-permute-done.3 = bf16[448,4096]{1,0:T(8,128)(2,1)} collective-permute-done((bf16[448,4096]{1,0:T(8,128)(2,1)}, bf16[448,4096]{1,0:T(8,128)(2,1)}, u32[]{:S(2)}, u32[]{:S(2)}) %collective-permute-start.3) | collective-permute-done | bytes 3670048 | tf_op jit(solution)/shard_map/ppermute | solution.py:10
  230.0 1.0 collective-permute-done.2
  231.0 14.4 %fusion.20 = bf16[1024,896]{1,0:T(8,128)(2,1)S(1)} fusion(bf16[448,4096]{1,0:T(8,128)(2,1)} %param.11, bf16[448,4096]{1,0:T(8,128)(2,1)} %collective-permute-done.3, pred[]{:T(512)S(6)} %eq.32, bf16[512,4096]{1,0:T(8,128)(2,1)} %maximum_select_fusion.4, bf16[512,4096]{1,0:T(8,128)(2,1)} %collective-permute-done.2, pred[]{:T(512)S(6)} %eq.29), kind=kOutput, calls=%fused_computation.35 | convolution fusion | flops 7587889152 | bytes 17563650 | tf_op jit(solution)/shard_map/dot_general | solution.py:74
  245.5 1.5 rev.18
  246.9 3.6 copy.27
  250.5 2.4 copy.28
  252.9 2.9 broadcast_select_fusion
  255.9 2.9 rev.19
  258.8 2.4 copy.30
  261.2 3.0 select_select_fusion.2
  264.2 2.9 rev.20
  267.1 3.6 copy.32
  270.7 3.6 copy.31
  274.3 0.8 select_select_fusion.1
  275.1 1.1 fusion.36
  276.2 0.6 copy.33
  276.8 2.2 collective-permute-done.4
  279.0 1.6 copy.34
  280.6 0.2 fusion.28
  280.8 3.5 collective-permute-start.5
  284.3 20.7 %collective-permute-done.5 = bf16[2,2,128,896]{2,3,1,0:T(8,128)(2,1)S(1)} collective-permute-done((bf16[2,2,128,896]{2,3,1,0:T(8,128)(2,1)S(1)}, bf16[2,2,128,896]{2,3,1,0:T(8,128)(2,1)S(1)}, u32[]{:S(2)}, u32[]{:S(2)}) %collective-permute-start.5) | collective-permute-done | bytes 917536 | tf_op jit(solution)/shard_map/ppermute | solution.py:10
  304.9 0.2 pad_maximum_fusion
  305.1 1.1 fusion.35
  306.2 3.1 collective-permute-start.6
  309.3 3.9 %copy.37 = bf16[128,7168]{0,1:T(8,128)(2,1)} copy(bf16[128,7168]{1,0:T(8,128)(2,1)} %param.9) | data formatting | bytes 3670016 | tf_op args[1]
  313.2 0.5 convolution_convert_fusion
  313.7 15.9 %collective-permute-done.6 = bf16[1,4,128,896]{2,3,1,0:T(8,128)(2,1)S(1)} collective-permute-done((bf16[1,4,128,896]{2,3,1,0:T(8,128)(2,1)}, bf16[1,4,128,896]{2,3,1,0:T(8,128)(2,1)S(1)}, u32[]{:S(2)}, u32[]{:S(2)}) %collective-permute-start.6) | collective-permute-done | bytes 917536 | tf_op jit(solution)/shard_map/ppermute | solution.py:10
  329.7 1.6 pad_maximum_fusion.1
  331.3 1.6 rev.21
  332.9 2.9 maximum_select_fusion.6
  335.9 2.9 rev.22
  338.7 2.9 select_select_fusion
  341.7 2.9 rev.23
  344.6 1.8 select_bitcast_fusion
  346.5 1.4 copy.36
  347.8 0.8 copy-done.3
  348.6 4.0 %multiply_reduce_fusion = (f32[]{:T(128)}, f32[64,64]{1,0:T(8,128)S(1)}) fusion(bf16[128,64]{0,1:T(8,128)(2,1)S(1)} %convolution_convert_fusion, bf16[7168,64]{0,1:T(8,128)(2,1)} %param.13, bf16[128,7168]{0,1:T(8,128)(2,1)S(1)} %copy-done.3, bf16[128,7168]{0,1:T(8,128)(2,1)} %bitcast.65), kind=kOutput, calls=%fused_computation.49 | convolution fusion | flops 125845504 | bytes 4620292 | tf_op jit(solution)/shard_map/esa,esb->eab/dot_general | solution.py:94
  353.3 0.1 reshape.191
  353.4 23.0 %all-gather = bf16[16,1,4096]{2,1,0:T(2,128)(2,1)S(1)} all-gather(bf16[1,1,4096]{2,1,0:T(2,128)(2,1)S(1)} %reshape.191), channel_id=1, replica_groups=mesh['ckpt'=2,'row'=16] {'row'}, dimensions={0}, use_global_device_ids=true | all-gather | bytes 139264 | tf_op jit(solution)/shard_map/all_gather | solution.py:102
  376.4 5.2 %convolution_select_fusion = f32[16,768]{1,0:T(8,128)} fusion(bf16[768,4096]{1,0:T(8,128)(2,1)} %param.14, bf16[16,1,4096]{2,1,0:T(2,128)(2,1)S(1)} %all-gather, s32[768]{0:T(1024)S(1)} %iota_add_fusion, s32[16]{0:T(128)S(1)} %copy-done.5), kind=kOutput, calls=%fused_computation.36 | convolution fusion | flops 100687872 | bytes 6474816 | tf_op jit(solution)/shard_map/dot_general | solution.py:101
  (14 shorter events, 0.0 us)
Async XLA Ops:
  0.0 313.2 %copy-start = (bf16[128,4096]{1,0:T(8,128)(2,1)S(1)}, bf16[128,4096]{1,0:T(8,128)(2,1)}, u32[]{:S(2)}) copy-start(bf16[128,4096]{1,0:T(8,128)(2,1)} %param.8) | copy-start | bytes 3145732
  0.0 3.1 collective-permute-start
  6.2 49.0 %collective-permute-start.1 = (bf16[256,4096]{1,0:T(8,128)(2,1)S(1)}, bf16[256,4096]{1,0:T(8,128)(2,1)}, u32[]{:S(2)}, u32[]{:S(2)}) collective-permute-start(bf16[256,4096]{1,0:T(8,128)(2,1)S(1)} %maximum_select_fusion.5), channel_id=1, source_target_pairs={{0,2},{1,3},{2,0},{3,1},{4,6},{5,7},{6,4},{7,5},{8,10},{9,11},{10,... | collective-permute-start | bytes 6291464 | tf_op jit(solution)/shard_map/ppermute | solution.py:10
  59.9 171.1 %collective-permute-start.2 = (bf16[512,4096]{1,0:T(8,128)(2,1)}, bf16[512,4096]{1,0:T(8,128)(2,1)}, u32[]{:S(2)}, u32[]{:S(2)}) collective-permute-start(bf16[512,4096]{1,0:T(8,128)(2,1)} %maximum_select_fusion.4), channel_id=1, source_target_pairs={{0,4},{1,5},{2,6},{3,7},{4,0},{5,1},{6,2},{7,3},{8,12},{9,13},{10,... | collective-permute-start | bytes 12582920 | tf_op jit(solution)/shard_map/ppermute | solution.py:10
  61.8 168.3 %collective-permute-start.3 = (bf16[448,4096]{1,0:T(8,128)(2,1)}, bf16[448,4096]{1,0:T(8,128)(2,1)}, u32[]{:S(2)}, u32[]{:S(2)}) collective-permute-start(bf16[448,4096]{1,0:T(8,128)(2,1)} %param.11), channel_id=1, source_target_pairs={{0,8},{1,9},{2,10},{3,11},{4,12},{5,13},{6,14},{7,15},{8,0},{9,1},... | collective-permute-start | bytes 11010056 | tf_op jit(solution)/shard_map/ppermute | solution.py:10
  276.2 2.8 collective-permute-start.4
  280.8 24.2 %collective-permute-start.5 = (bf16[2,2,128,896]{2,3,1,0:T(8,128)(2,1)S(1)}, bf16[2,2,128,896]{2,3,1,0:T(8,128)(2,1)S(1)}, u32[]{:S(2)}, u32[]{:S(2)}) collective-permute-start(bf16[2,2,128,896]{2,3,1,0:T(8,128)(2,1)S(1)} %get-tuple-element.8), channel_id=1, source_target_pairs={{0,2},{1,3},{2,0},{3,1},{4,6},{5,7},{6,4},{7,5},{8,10},{9,11},{10,... | collective-permute-start | bytes 2752520 | tf_op jit(solution)/shard_map/ppermute | solution.py:10
  306.2 23.5 %copy-start.1 = (bf16[1,1,4,128,896]{3,4,2,1,0:T(8,128)(2,1)}, bf16[1,1,4,128,896]{3,4,2,1,0:T(8,128)(2,1)S(1)}, u32[]{:S(2)}) copy-start(bf16[1,1,4,128,896]{3,4,2,1,0:T(8,128)(2,1)S(1)} %get-tuple-element.5) | copy-start | bytes 2752516
  306.2 7.1 %copy-start.4 = (bf16[4096,64]{0,1:T(8,128)(2,1)S(1)}, bf16[4096,64]{0,1:T(8,128)(2,1)}, u32[]{:S(2)}) copy-start(bf16[4096,64]{0,1:T(8,128)(2,1)} %param.12) | copy-start | bytes 1572868
  306.2 23.5 %collective-permute-start.6 = (bf16[1,4,128,896]{2,3,1,0:T(8,128)(2,1)}, bf16[1,4,128,896]{2,3,1,0:T(8,128)(2,1)S(1)}, u32[]{:S(2)}, u32[]{:S(2)}) collective-permute-start(bf16[1,4,128,896]{2,3,1,0:T(8,128)(2,1)} %get-tuple-element.6), channel_id=1, source_target_pairs={{0,4},{1,5},{2,6},{3,7},{4,0},{5,1},{6,2},{7,3},{8,12},{9,13},{10,... | collective-permute-start | bytes 2752520 | tf_op jit(solution)/shard_map/ppermute | solution.py:10
  329.7 1.6 copy-start.2
  346.5 2.2 copy-start.3
  348.6 27.8 %copy-start.5 = (s32[16]{0:T(128)S(1)}, s32[16]{0:T(128)}, u32[]{:S(2)}) copy-start(s32[16]{0:T(128)} %param.15) | copy-start | bytes 196
where the time goes:
time: 382 us
  waiting for transfers between devices  254 us (66%)
  local copies, waits for them, and re-layouts  40.9 us (11%)
  other arithmetic  24.3 us (6%)
  matrix products  24 us (6%)
  blocking collectives  23 us (6%)
  starting transfers between devices  14.5 us (4%)
    ppermute x7, waiting for transfers between devices, partner(): lax.ppermute(value, axis, [(i, i ^ 1 << bit) for i in range(lax.axis_size...  254 us
    all_gather x1, blocking collectives, shards(): lax.all_gather(queries, 'row', axis=0, tiled=True)  23 us
    rev x7, local copies, waits for them, and re-layouts, xor_order(): flipped = shaped[:, ::-1].reshape(slot_data.shape)  18.3 us
    ppermute x7, starting transfers between devices, partner(): lax.ppermute(value, axis, [(i, i ^ 1 << bit) for i in range(lax.axis_size...  14.5 us
    dot_general x1, matrix products, shards(): lax.dot_general(grad_group, weights_lane, (((1,), (1,)), ((), ())), prefe...  14.4 us
    select_n x5, other arithmetic, xor_order(): slot_data = jnp.where(lane_id >> bit_level & 1 == 1, flipped, slot_data)  12.6 us
    select_n x2, other arithmetic, collect(): jnp.where(upper_half, jnp.concatenate([partner_rows, pieces], axis=0), jn...  7.89 us
  transfers between devices with their start and end apart: 7, of which 7 were waited for; matrix products, arithmetic and copies ran while one was open for 1% of the time, Pallas kernels for 0%

commit v1 on v0

--- a/solution.py
+++ b/solution.py
@@ -4,6 +4,18 @@
 from jax.sharding import PartitionSpec as P
 
 SEQ_LEN = 128
+
+
+def gather_by_bits(value, axis, dim):
+    ways, here = (lax.axis_size(axis), lax.axis_index(axis))
+    grown, reach = (value, 1)
+    while reach < ways:
+        theirs = lax.ppermute(grown, axis, [(d, d ^ reach) for d in range(ways)])
+        mine_first = jnp.concatenate([grown, theirs], axis=dim)
+        theirs_first = jnp.concatenate([theirs, grown], axis=dim)
+        grown = jnp.where(here & reach == 0, mine_first, theirs_first)
+        reach = 2 * reach
+    return grown
 
 
 def partner(value, axis, bit):
@@ -99,7 +111,7 @@
     stored_rows = stored.shape[0]
     column = position * stored_rows + jnp.arange(stored_rows, dtype=jnp.int32)
     products = lax.dot_general(
-        lax.all_gather(queries, "row", axis=0, tiled=True),
+        gather_by_bits(queries, "row", 0),
         stored,
         (((1,), (1,)), ((), ())),
         preferred_element_type=jnp.float32,

time: 382 us -> 374 us (0.979)
  blocking collectives: 23 us -> 0 us
  waiting for transfers between devices: 254 us -> 263 us
  starting transfers between devices: 14.5 us -> 21.1 us
    all_gather x1 -> x0, blocking collectives: 23 us -> none  [shards(): lax.all_gather(queries, 'row', axis=0, tiled=True)]
    ppermute x0 -> x4, waiting for transfers between devices: none -> 8.37 us  [gather_by_bits(): theirs = lax.ppermute(grown, axis, [(d, d ^ reach) for d in range(ways)])]
    ppermute x0 -> x4, starting transfers between devices: none -> 6.61 us  [gather_by_bits(): theirs = lax.ppermute(grown, axis, [(d, d ^ reach) for d in range(ways)])]
  transfers between devices with their start and end apart: 7 -> 11, of which waited for: 7 -> 11; matrix products, arithmetic and copies ran while one was open for 1% -> 1% of each run, Pallas kernels for 0% -> 0%
where the time goes in v1:
time: 374 us; the launch traced here: 373 us
  waiting for transfers between devices  263 us (70%)
  local copies, waits for them, and re-layouts  40.8 us (11%)
  other arithmetic  24.5 us (7%)
  matrix products  23.7 us (6%)
  starting transfers between devices  21.1 us (6%)
    ppermute x7, waiting for transfers between devices, partner(): lax.ppermute(value, axis, [(i, i ^ 1 << bit) for i in range(lax.axis_size...  254 us
    rev x7, local copies, waits for them, and re-layouts, xor_order(): flipped = shaped[:, ::-1].reshape(slot_data.shape)  18.3 us
    ppermute x7, starting transfers between devices, partner(): lax.ppermute(value, axis, [(i, i ^ 1 << bit) for i in range(lax.axis_size...  14.5 us
    dot_general x1, matrix products, shards(): lax.dot_general(grad_group, weights_lane, (((1,), (1,)), ((), ())), prefe...  14.4 us
    select_n x5, other arithmetic, xor_order(): slot_data = jnp.where(lane_id >> bit_level & 1 == 1, flipped, slot_data)  12.6 us
    ppermute x4, waiting for transfers between devices, gather_by_bits(): theirs = lax.ppermute(grown, axis, [(d, d ^ reach) for d in range(ways)])  8.37 us
    select_n x2, other arithmetic, collect(): jnp.where(upper_half, jnp.concatenate([partner_rows, pieces], axis=0), jn...  7.88 us
  transfers between devices with their start and end apart: 11, of which 11 were waited for; matrix products, arithmetic and copies ran while one was open for 1% of the time, Pallas kernels for 0%

profile of v1, /device:TPU:0, one launch (start us, length us, event | category | flops | bytes accessed | tf_op | source)
XLA Modules:
  0.0 373.4 jit_solution(16664685154786710187)
XLA Ops:
  0.5 2.6 collective-permute-done
  3.1 3.1 maximum_select_fusion.5
  6.2 2.9 collective-permute-start.1
  9.2 46.0 %collective-permute-done.1 = bf16[256,4096]{1,0:T(8,128)(2,1)} collective-permute-done((bf16[256,4096]{1,0:T(8,128)(2,1)S(1)}, bf16[256,4096]{1,0:T(8,128)(2,1)}, u32[]{:S(2)}, u32[]{:S(2)}) %collective-permute-start.1) | collective-permute-done | bytes 2097184 | tf_op jit(solution)/shard_map/ppermute | solution.py:22
  55.2 4.7 %maximum_select_fusion.4 = bf16[512,4096]{1,0:T(8,128)(2,1)} fusion(bf16[256,4096]{1,0:T(8,128)(2,1)S(1)} %maximum_select_fusion.5, bf16[256,4096]{1,0:T(8,128)(2,1)} %collective-permute-done.1, pred[]{:T(512)S(6)} %eq.46), kind=kLoop, calls=%fused_computation.17 | loop fusion | flops 18874368 | bytes 8388609 | tf_op jit(solution)/shard_map/jit(_where)/select_n | solution.py:29
  59.9 1.8 collective-permute-start.2
  61.8 2.6 collective-permute-start.3
  64.4 165.7 %collective-permute-done.3 = bf16[448,4096]{1,0:T(8,128)(2,1)} collective-permute-done((bf16[448,4096]{1,0:T(8,128)(2,1)}, bf16[448,4096]{1,0:T(8,128)(2,1)}, u32[]{:S(2)}, u32[]{:S(2)}) %collective-permute-start.3) | collective-permute-done | bytes 3670048 | tf_op jit(solution)/shard_map/ppermute | solution.py:22
  230.0 1.0 collective-permute-done.2
  231.0 14.4 %fusion.20 = bf16[1024,896]{1,0:T(8,128)(2,1)S(1)} fusion(bf16[448,4096]{1,0:T(8,128)(2,1)} %param.11, bf16[448,4096]{1,0:T(8,128)(2,1)} %collective-permute-done.3, pred[]{:T(512)S(6)} %eq.48, bf16[512,4096]{1,0:T(8,128)(2,1)} %maximum_select_fusion.4, bf16[512,4096]{1,0:T(8,128)(2,1)} %collective-permute-done.2, pred[]{:T(512)S(6)} %eq.45), kind=kOutput, calls=%fused_computation.35 | convolution fusion | flops 7587889152 | bytes 17563650 | tf_op jit(solution)/shard_map/dot_general | solution.py:86
  245.4 1.5 rev.18
  246.9 3.6 copy.15
  250.5 2.4 copy.16
  252.9 3.0 broadcast_select_fusion
  255.9 2.9 rev.19
  258.8 2.4 copy.18
  261.2 3.0 select_select_fusion.2
  264.2 2.9 rev.20
  267.1 3.6 copy.20
  270.7 3.6 copy.19
  274.3 0.8 select_select_fusion.1
  275.1 1.1 fusion.41
  276.8 2.2 collective-permute-done.4
  279.0 1.6 copy.22
  280.7 3.5 collective-permute-start.5
  284.3 20.7 %collective-permute-done.5 = bf16[2,2,128,896]{2,3,1,0:T(8,128)(2,1)S(1)} collective-permute-done((bf16[2,2,128,896]{2,3,1,0:T(8,128)(2,1)S(1)}, bf16[2,2,128,896]{2,3,1,0:T(8,128)(2,1)S(1)}, u32[]{:S(2)}, u32[]{:S(2)}) %collective-permute-start.5) | collective-permute-done | bytes 917536 | tf_op jit(solution)/shard_map/ppermute | solution.py:22
  305.1 1.0 fusion.40
  306.1 3.2 collective-permute-start.6
  309.3 3.9 %copy.25 = bf16[128,7168]{0,1:T(8,128)(2,1)} copy(bf16[128,7168]{1,0:T(8,128)(2,1)} %param.9) | data formatting | bytes 3670016 | tf_op args[1]
  313.6 16.0 %collective-permute-done.6 = bf16[1,4,128,896]{2,3,1,0:T(8,128)(2,1)S(1)} collective-permute-done((bf16[1,4,128,896]{2,3,1,0:T(8,128)(2,1)}, bf16[1,4,128,896]{2,3,1,0:T(8,128)(2,1)S(1)}, u32[]{:S(2)}, u32[]{:S(2)}) %collective-permute-start.6) | collective-permute-done | bytes 917536 | tf_op jit(solution)/shard_map/ppermute | solution.py:22
  329.6 1.6 pad_maximum_fusion.1
  331.2 1.6 rev.21
  332.8 2.9 maximum_select_fusion.6
  335.8 2.9 rev.22
  338.7 2.9 select_select_fusion
  341.6 2.9 rev.23
  344.6 1.8 select_bitcast_fusion
  346.4 1.4 copy.24
  347.8 0.8 copy-done.3
  348.6 3.7 multiply_reduce_fusion
  353.1 1.2 collective-permute-done.7
  354.4 2.6 collective-permute-start.8
  356.9 1.7 collective-permute-done.8
  358.7 2.4 collective-permute-start.9
  361.1 1.9 collective-permute-done.9
  363.1 1.6 collective-permute-start.10
  364.7 3.6 collective-permute-done.10
  368.3 5.1 %convolution_select_fusion = f32[16,768]{1,0:T(8,128)} fusion(bf16[768,4096]{1,0:T(8,128)(2,1)} %param.14, bf16[8,4096]{1,0:T(8,128)(2,1)S(1)} %collective-permute-done.10, bf16[8,4096]{1,0:T(8,128)(2,1)S(1)} %maximum_select_fusion.13, pred[]{:T(512)S(6)} %eq.38, s32[768]{0:T(1024)S(1)} %iota_add_fusion, s32[16]{0:T(128)S(1)} %copy-done.5), kind=kOutput, calls=%fused_computation.37 | convolution fusion | flops 101277696 | bytes 6474817 | tf_op jit(solution)/shard_map/dot_general | solution.py:113
  (24 shorter events, 2.2 us)
Async XLA Ops:
  0.0 313.2 %copy-start = (bf16[128,4096]{1,0:T(8,128)(2,1)S(1)}, bf16[128,4096]{1,0:T(8,128)(2,1)}, u32[]{:S(2)}) copy-start(bf16[128,4096]{1,0:T(8,128)(2,1)} %param.8) | copy-start | bytes 3145732
  0.0 3.1 collective-permute-start
  6.2 49.0 %collective-permute-start.1 = (bf16[256,4096]{1,0:T(8,128)(2,1)S(1)}, bf16[256,4096]{1,0:T(8,128)(2,1)}, u32[]{:S(2)}, u32[]{:S(2)}) collective-permute-start(bf16[256,4096]{1,0:T(8,128)(2,1)S(1)} %maximum_select_fusion.5), channel_id=1, source_target_pairs={{0,2},{1,3},{2,0},{3,1},{4,6},{5,7},{6,4},{7,5},{8,10},{9,11},{10,... | collective-permute-start | bytes 6291464 | tf_op jit(solution)/shard_map/ppermute | solution.py:22
  59.9 171.1 %collective-permute-start.2 = (bf16[512,4096]{1,0:T(8,128)(2,1)}, bf16[512,4096]{1,0:T(8,128)(2,1)}, u32[]{:S(2)}, u32[]{:S(2)}) collective-permute-start(bf16[512,4096]{1,0:T(8,128)(2,1)} %maximum_select_fusion.4), channel_id=1, source_target_pairs={{0,4},{1,5},{2,6},{3,7},{4,0},{5,1},{6,2},{7,3},{8,12},{9,13},{10,... | collective-permute-start | bytes 12582920 | tf_op jit(solution)/shard_map/ppermute | solution.py:22
  61.8 168.3 %collective-permute-start.3 = (bf16[448,4096]{1,0:T(8,128)(2,1)}, bf16[448,4096]{1,0:T(8,128)(2,1)}, u32[]{:S(2)}, u32[]{:S(2)}) collective-permute-start(bf16[448,4096]{1,0:T(8,128)(2,1)} %param.11), channel_id=1, source_target_pairs={{0,8},{1,9},{2,10},{3,11},{4,12},{5,13},{6,14},{7,15},{8,0},{9,1},... | collective-permute-start | bytes 11010056 | tf_op jit(solution)/shard_map/ppermute | solution.py:22
  276.2 2.8 collective-permute-start.4
  280.7 24.2 %collective-permute-start.5 = (bf16[2,2,128,896]{2,3,1,0:T(8,128)(2,1)S(1)}, bf16[2,2,128,896]{2,3,1,0:T(8,128)(2,1)S(1)}, u32[]{:S(2)}, u32[]{:S(2)}) collective-permute-start(bf16[2,2,128,896]{2,3,1,0:T(8,128)(2,1)S(1)} %get-tuple-element.8), channel_id=1, source_target_pairs={{0,2},{1,3},{2,0},{3,1},{4,6},{5,7},{6,4},{7,5},{8,10},{9,11},{10,... | collective-permute-start | bytes 2752520 | tf_op jit(solution)/shard_map/ppermute | solution.py:22
  306.1 23.5 %copy-start.1 = (bf16[1,1,4,128,896]{3,4,2,1,0:T(8,128)(2,1)}, bf16[1,1,4,128,896]{3,4,2,1,0:T(8,128)(2,1)S(1)}, u32[]{:S(2)}) copy-start(bf16[1,1,4,128,896]{3,4,2,1,0:T(8,128)(2,1)S(1)} %get-tuple-element.5) | copy-start | bytes 2752516
  306.1 7.0 %copy-start.4 = (bf16[4096,64]{0,1:T(8,128)(2,1)S(1)}, bf16[4096,64]{0,1:T(8,128)(2,1)}, u32[]{:S(2)}) copy-start(bf16[4096,64]{0,1:T(8,128)(2,1)} %param.12) | copy-start | bytes 1572868
  306.1 23.5 %collective-permute-start.6 = (bf16[1,4,128,896]{2,3,1,0:T(8,128)(2,1)}, bf16[1,4,128,896]{2,3,1,0:T(8,128)(2,1)S(1)}, u32[]{:S(2)}, u32[]{:S(2)}) collective-permute-start(bf16[1,4,128,896]{2,3,1,0:T(8,128)(2,1)} %get-tuple-element.6), channel_id=1, source_target_pairs={{0,4},{1,5},{2,6},{3,7},{4,0},{5,1},{6,2},{7,3},{8,12},{9,13},{10,... | collective-permute-start | bytes 2752520 | tf_op jit(solution)/shard_map/ppermute | solution.py:22
  329.6 1.6 copy-start.2
  346.4 2.2 copy-start.3
  348.6 19.7 %copy-start.5 = (s32[16]{0:T(128)S(1)}, s32[16]{0:T(128)}, u32[]{:S(2)}) copy-start(s32[16]{0:T(128)} %param.15) | copy-start | bytes 196
  353.1 1.2 collective-permute-start.7
  354.4 4.3 %collective-permute-start.8 = (bf16[2,4096]{1,0:T(2,128)(2,1)S(1)}, bf16[2,4096]{1,0:T(2,128)(2,1)S(1)}, u32[]{:S(2)}, u32[]{:S(2)}) collective-permute-start(bf16[2,4096]{1,0:T(2,128)(2,1)S(1)} %broadcast_select_fusion.1), channel_id=1, source_target_pairs={{0,2},{1,3},{2,0},{3,1},{4,6},{5,7},{6,4},{7,5},{8,10},{9,11},{10,... | collective-permute-start | bytes 49160 | tf_op jit(solution)/shard_map/ppermute | solution.py:13
  358.7 4.3 %collective-permute-start.9 = (bf16[4,4096]{1,0:T(4,128)(2,1)S(1)}, bf16[4,4096]{1,0:T(4,128)(2,1)S(1)}, u32[]{:S(2)}, u32[]{:S(2)}) collective-permute-start(bf16[4,4096]{1,0:T(4,128)(2,1)S(1)} %maximum_select_fusion.14), channel_id=1, source_target_pairs={{0,4},{1,5},{2,6},{3,7},{4,0},{5,1},{6,2},{7,3},{8,12},{9,13},{10,... | collective-permute-start | bytes 98312 | tf_op jit(solution)/shard_map/ppermute | solution.py:13
  363.1 5.2 %collective-permute-start.10 = (bf16[8,4096]{1,0:T(8,128)(2,1)S(1)}, bf16[8,4096]{1,0:T(8,128)(2,1)S(1)}, u32[]{:S(2)}, u32[]{:S(2)}) collective-permute-start(bf16[8,4096]{1,0:T(8,128)(2,1)S(1)} %maximum_select_fusion.13), channel_id=1, source_target_pairs={{0,8},{1,9},{2,10},{3,11},{4,12},{5,13},{6,14},{7,15},{8,0},{9,1},... | collective-permute-start | bytes 196616 | tf_op jit(solution)/shard_map/ppermute | solution.py:13
